TPU v7x, 256 devices: a whole 4x4x8 slice. The times are simulated.
256 devices in a mesh: rows: 32 (over y, z), tensor: 8 (over x, core).
Axes of the slice: x: 4, y: 4, z: 8, core: 2. Of those that a mesh axis runs over, the one named last changes fastest.
Arguments:
- token_ids: int32 [256, 4], replicated, may hold values from 0 to 65535
- cache_lengths: int32 [256], P('rows'), may hold values from 160 to 1280, as said below
- doc_ids: int32 [256], replicated, may hold values from 0 to 31
- embed_table: bfloat16 [65536, 8192], P('tensor', 'rows'), may hold values from -10.5 to 10.5
- cache_keys: bfloat16 [256, 1280, 1024], P('rows', None, 'tensor'), may hold values from -700 to 700
- cache_values: bfloat16 [256, 1280, 1024], P('rows', None, 'tensor'), may hold values from -6 to 6
- decode_gain: float32 [8192], P('rows'), may hold values from 0.1 to 1.9
- decode_query: bfloat16 [8192, 8192], P('rows', 'tensor'), may hold values from -0.0625 to 0.0625
- decode_key: bfloat16 [8192, 1024], P('rows', 'tensor'), may hold values from -0.0625 to 0.0625
- decode_value: bfloat16 [8192, 1024], P('rows', 'tensor'), may hold values from -0.0625 to 0.0625
- decode_out: bfloat16 [8192, 8192], P('tensor', 'rows'), may hold values from -0.0625 to 0.0625
- reduce_gain: float32 [8192], P('rows'), may hold values from 0.8 to 10
- reduce_query: bfloat16 [8192, 8192], P('rows', 'tensor'), may hold values from -0.0625 to 0.0625
- reduce_key: bfloat16 [8192, 1024], P('rows', 'tensor'), may hold values from -0.0625 to 0.0625
- reduce_value: bfloat16 [8192, 1024], P('rows', 'tensor'), may hold values from -0.0625 to 0.0625
- reduce_out: bfloat16 [8192, 8192], P('tensor', 'rows'), may hold values from -0.0625 to 0.0625
Outputs:
- reduced: bfloat16 [1024, 8192], P(None, 'rows')
Inputs may be any that keep to these rules, and one draw needn't show every extreme that they name: Passage row c holds cache entries at positions below cache_lengths[c]; one row in every draw has a full cache of 1280.
All inputs are finite; a program needn't handle non-finite values.
Results may differ from a plain program's by a relative error of at most 0.035.
The roundings to bfloat16 on the way count: a program that leaves them out, or rounds other values in their place, can miss the bound.
Values may be sent and summed in bfloat16 or wider, within the bound.
A program may use at most 64 MiB of HBM per device.

v0:
```python
import jax
import jax.numpy as jnp
from jax import lax
from jax.sharding import PartitionSpec as P

D = 8192
HEAD_DIM = 128
EPSILON = 1e-05
ROPE_BASE = 500000.0


def rotate(vectors, positions):
    half_dim = vectors.shape[-1] // 2
    frequencies = ROPE_BASE ** (-2.0 * jnp.arange(half_dim, dtype=jnp.float32) / vectors.shape[-1])
    angles = positions.astype(jnp.float32)[..., None] * frequencies
    cosine = jnp.cos(angles)
    sine_part = jnp.sin(angles)
    lower_half = vectors[..., :half_dim]
    upper_half = vectors[..., half_dim:]
    return jnp.concatenate(
        [
            lower_half * cosine - upper_half * sine_part,
            upper_half * cosine + lower_half * sine_part,
        ],
        axis=-1,
    )


def width_total(partial_value):
    return lax.psum(partial_value, "tensor")


def row_scale(summed):
    return lax.rsqrt(summed / D + EPSILON)


def head_terms(normed, matrices, squares, groups):
    partial = jnp.concatenate(
        [jnp.dot(normed, matrix, preferred_element_type=jnp.float32) for matrix in matrices], axis=1
    )
    tokens, cols = partial.shape
    own = tokens // groups
    payload = jnp.concatenate(
        [partial.reshape(groups, own * cols), squares.reshape(groups, own)], axis=1
    ).reshape(groups, 8, (own * cols + own) // 8)
    summed = lax.psum_scatter(payload, "rows", scatter_dimension=0, tiled=True)
    summed = summed.reshape(own * cols + own)
    return (summed[: own * cols].reshape(own, cols), summed[own * cols :])


def head_mix(attended, matrix):
    return jnp.dot(
        lax.all_gather(attended, "rows", axis=0, tiled=True),
        matrix,
        preferred_element_type=jnp.float32,
    )


def per_device(
    token_ids,
    cache_lengths,
    doc_ids,
    embed_table,
    cache_keys,
    cache_values,
    decode_gain,
    decode_query,
    decode_key,
    decode_value,
    decode_out,
    reduce_gain,
    reduce_query,
    reduce_key,
    reduce_value,
    reduce_out,
):
    step_count = token_ids.shape[1]
    passage_count = token_ids.shape[0]
    token_count = passage_count * step_count
    own_passages = cache_lengths.shape[0]
    own_tokens = own_passages * step_count
    row_first = lax.axis_index("rows") * own_tokens
    query_cols = decode_query.shape[1]
    kv_cols = decode_key.shape[1]
    local_heads = query_cols // HEAD_DIM
    local_kv = kv_cols // HEAD_DIM
    group_size = local_heads // local_kv
    score_scale = HEAD_DIM ** (-0.5)
    step_ids = jnp.arange(step_count, dtype=jnp.int32)
    vocab_part = embed_table.shape[0]
    local_ids = token_ids.reshape(token_count) - lax.axis_index("tensor") * vocab_part
    inside = (local_ids >= 0) & (local_ids < vocab_part)
    picked = jnp.take(embed_table, jnp.clip(local_ids, 0, vocab_part - 1), axis=0)
    picked = jnp.where(inside[:, None], picked, jnp.zeros_like(picked))
    embedded = width_total(picked).astype(jnp.float32)
    row_groups = token_count // own_tokens
    normed = (embedded * decode_gain[None, :]).astype(jnp.bfloat16)
    projected, dec_squares = head_terms(
        normed,
        (decode_query, decode_key, decode_value),
        jnp.sum(embedded * embedded, axis=1),
        row_groups,
    )
    projected = projected * row_scale(dec_squares)[:, None]
    positions = (cache_lengths[:, None] + step_ids[None, :]).reshape(own_tokens, 1)
    queries = rotate(
        projected[:, :query_cols].reshape(own_tokens, local_heads, HEAD_DIM), positions
    ).astype(jnp.bfloat16)
    keys_new = rotate(
        projected[:, query_cols : query_cols + kv_cols].reshape(own_tokens, local_kv, HEAD_DIM),
        positions,
    ).astype(jnp.bfloat16)
    values_new = projected[:, query_cols + kv_cols :].astype(jnp.bfloat16)
    queries = queries.reshape(own_passages, step_count, local_kv, group_size, HEAD_DIM)
    keys_new = keys_new.reshape(own_passages, step_count, local_kv, HEAD_DIM)
    values_new = values_new.reshape(own_passages, step_count, local_kv, HEAD_DIM)
    capacity = cache_keys.shape[1]
    keys_old = cache_keys.reshape(own_passages, capacity, local_kv, HEAD_DIM)
    values_old = cache_values.reshape(own_passages, capacity, local_kv, HEAD_DIM)
    new_scores = (
        jnp.einsum("rskgd,rtkd->rskgt", queries, keys_new, preferred_element_type=jnp.float32)
        * score_scale
    )
    causal = step_ids[None, :] <= step_ids[:, None]
    new_scores = jnp.where(causal[None, :, None, None, :], new_scores, -jnp.inf)
    old_scores = (
        jnp.einsum("rskgd,rckd->rskgc", queries, keys_old, preferred_element_type=jnp.float32)
        * score_scale
    )
    slot_ids = jnp.arange(capacity, dtype=jnp.int32)
    live_mask = slot_ids[None, :] < cache_lengths[:, None]
    old_scores = jnp.where(live_mask[:, None, None, None, :], old_scores, -jnp.inf)
    highest = jnp.maximum(jnp.max(old_scores, axis=-1), jnp.max(new_scores, axis=-1))
    old_exp = jnp.exp(old_scores - highest[..., None])
    new_exp = jnp.exp(new_scores - highest[..., None])
    summed = jnp.sum(old_exp, axis=-1) + jnp.sum(new_exp, axis=-1)
    old_weights = (old_exp / summed[..., None]).astype(jnp.bfloat16)
    new_weights = (new_exp / summed[..., None]).astype(jnp.bfloat16)
    attended = jnp.einsum(
        "rskgc,rckd->rskgd", old_weights, values_old, preferred_element_type=jnp.float32
    )
    attended = attended + jnp.einsum(
        "rskgt,rtkd->rskgd", new_weights, values_new, preferred_element_type=jnp.float32
    )
    attended = attended.reshape(own_tokens, query_cols).astype(jnp.bfloat16)
    partial_value = head_mix(attended, decode_out)
    summary = (embedded + width_total(partial_value)).astype(jnp.bfloat16)
    summary_wide = summary.astype(jnp.float32)
    normed_red = (summary_wide * reduce_gain[None, :]).astype(jnp.bfloat16)
    passage_index = jnp.arange(passage_count, dtype=jnp.int32)
    earlier = jnp.sum(
        (
            (doc_ids[None, :] == doc_ids[:, None])
            & (passage_index[None, :] < passage_index[:, None])
        ).astype(jnp.int32),
        axis=1,
    )
    doc_positions = (earlier[:, None] * step_count + step_ids[None, :]).reshape(token_count, 1)
    doc_tokens = (doc_ids[:, None] + jnp.zeros_like(step_ids)[None, :]).reshape(token_count)
    own_positions = lax.dynamic_slice_in_dim(doc_positions, row_first, own_tokens, 0)
    projected, red_squares = head_terms(
        normed_red,
        (reduce_query, reduce_key, reduce_value),
        jnp.sum(summary_wide * summary_wide, axis=1),
        row_groups,
    )
    projected = projected * row_scale(red_squares)[:, None]
    queries_red = rotate(
        projected[:, :query_cols].reshape(own_tokens, local_heads, HEAD_DIM), own_positions
    ).astype(jnp.bfloat16)
    keys_own = (
        rotate(
            projected[:, query_cols : query_cols + kv_cols].reshape(own_tokens, local_kv, HEAD_DIM),
            own_positions,
        )
        .astype(jnp.bfloat16)
        .reshape(own_tokens, kv_cols)
    )
    values_own = projected[:, query_cols + kv_cols :].astype(jnp.bfloat16)
    kv_red = lax.all_gather(
        jnp.concatenate([keys_own, values_own], axis=1), "rows", axis=0, tiled=True
    )
    keys_red, values_red = (kv_red[:, :kv_cols], kv_red[:, kv_cols:])
    queries_red = queries_red.reshape(own_tokens, local_kv, group_size, HEAD_DIM)
    keys_red = keys_red.reshape(token_count, local_kv, HEAD_DIM)
    values_red = values_red.reshape(token_count, local_kv, HEAD_DIM)
    token_index = jnp.arange(token_count, dtype=jnp.int32)
    own_index = row_first + jnp.arange(own_tokens, dtype=jnp.int32)
    own_docs = lax.dynamic_slice_in_dim(doc_tokens, row_first, own_tokens, 0)
    allowed = (own_docs[:, None] == doc_tokens[None, :]) & (
        token_index[None, :] <= own_index[:, None]
    )
    red_scores = (
        jnp.einsum("tkgd,ukd->tkgu", queries_red, keys_red, preferred_element_type=jnp.float32)
        * score_scale
    )
    red_scores = jnp.where(allowed[:, None, None, :], red_scores, -jnp.inf)
    red_high = jnp.max(red_scores, axis=-1)
    red_exp = jnp.exp(red_scores - red_high[..., None])
    red_weights = (red_exp / jnp.sum(red_exp, axis=-1)[..., None]).astype(jnp.bfloat16)
    red_out = jnp.einsum(
        "tkgu,ukd->tkgd", red_weights, values_red, preferred_element_type=jnp.float32
    )
    red_out = red_out.reshape(own_tokens, query_cols).astype(jnp.bfloat16)
    return (summary_wide + width_total(head_mix(red_out, reduce_out))).astype(jnp.bfloat16)


def solution(mesh):
    return jax.shard_map(
        per_device,
        mesh=mesh,
        in_specs=(
            P(),
            P("rows"),
            P(),
            P("tensor", "rows"),
            P("rows", None, "tensor"),
            P("rows", None, "tensor"),
            P("rows"),
            P("rows", "tensor"),
            P("rows", "tensor"),
            P("rows", "tensor"),
            P("tensor", "rows"),
            P("rows"),
            P("rows", "tensor"),
            P("rows", "tensor"),
            P("rows", "tensor"),
            P("tensor", "rows"),
        ),
        out_specs=P(None, "rows"),
        check_vma=False,
    )
```

profile of v0, /device:TPU:8, one launch (start us, length us, event | category | flops | bytes accessed | tf_op | source)
XLA Modules:
  0.0 927.0 jit_solution(14804765056638584329)
XLA Ops:
  6.5 0.9 subtract_clamp_fusion
  8.8 6.2 gather_fusion
  15.0 1.1 select_select_fusion
  16.3 69.0 %all-reduce.6.cloned.1.call-done = bf16[1024,256]{1,0:T(8,128)(2,1)} async-done(((bf16[1024,256]{1,0:T(8,128)(2,1)}), bf16[1024,256]{1,0:T(8,128)(2,1)}) %all-reduce.6.cloned.1.call-update) | async-done | bytes 524304 | tf_op jit(solution)/shard_map/psum | solution.py:30
  85.3 2.0 fusion.41
  88.0 2.8 pad_maximum_fusion.2
  90.8 5.9 copy.36
  96.7 5.6 reshape.597
  102.5 5.2 pad_maximum_fusion
  107.7 6.8 reshape.599
  116.9 209.4 %reduce-scatter.7.cloned.1.call-done = f32[1,8,5124]{2,1,0:T(8,128)} async-done(((f32[32,8,5124]{2,1,0:T(8,128)}), f32[1,8,5124]{2,1,0:T(8,128)}) %reduce-scatter.7.cloned.1.call-update) | async-done | bytes 163984
  326.3 1.0 reshape.600
  327.9 0.9 broadcast_multiply_fusion.1
  328.9 0.8 fusion.65
  329.9 1.1 fusion.81
  333.5 76.0 %all-gather.3.cloned.1.call-done = bf16[1024,1024]{1,0:T(8,128)(2,1)} async-done(((bf16[32,1024]{1,0:T(8,128)(2,1)}), bf16[1024,1024]{1,0:T(8,128)(2,1)}) %all-gather.3.cloned.1.call-update) | async-done | bytes 2097168 | tf_op jit(solution)/shard_map/all_gather | solution.py:53
  409.5 3.3 fusion.84
  413.0 66.1 %all-reduce.8.cloned.1.call-done = f32[1024,256]{1,0:T(8,128)} async-done(((f32[1024,256]{1,0:T(8,128)}), f32[1024,256]{1,0:T(8,128)}) %all-reduce.8.cloned.1.call-update) | async-done | bytes 1048592 | tf_op jit(solution)/shard_map/psum | solution.py:30
  479.1 1.4 fusion.25
  480.6 0.8 fusion.35
  482.1 2.9 pad_maximum_fusion.3
  485.1 5.9 copy.37
  491.0 5.6 reshape.607
  496.6 5.2 pad_maximum_fusion.1
  501.8 6.8 reshape.609
  509.6 211.0 %reduce-scatter.9.cloned.1.call-done = f32[1,8,5124]{2,1,0:T(8,128)} async-done(((f32[32,8,5124]{2,1,0:T(8,128)}), f32[1,8,5124]{2,1,0:T(8,128)}) %reduce-scatter.9.cloned.1.call-update) | async-done | bytes 163984
  720.6 1.0 reshape.610
  722.1 47.8 %all_gather.10 = bf16[1024,256]{1,0:T(8,128)(2,1)S(1)} all-gather(bf16[32,256]{1,0:T(8,128)(2,1)S(1)} %pad_maximum_fusion.5), channel_id=1, replica_groups=mesh['rows'=32,'tensor'=8] {'rows'}, dimensions={0}, use_global_device_ids=true | all-gather | bytes 540672 | tf_op jit(solution)/shard_map/all_gather | solution.py:180
  771.9 76.5 %all-gather.5.cloned.1.call-done = bf16[1024,1024]{1,0:T(8,128)(2,1)} async-done(((bf16[32,1024]{1,0:T(8,128)(2,1)}), bf16[1024,1024]{1,0:T(8,128)(2,1)}) %all-gather.5.cloned.1.call-update) | async-done | bytes 2097168 | tf_op jit(solution)/shard_map/all_gather | solution.py:53
  848.4 3.4 fusion.85
  851.8 66.3 %all-reduce.10.cloned.1.call-done = f32[1024,256]{1,0:T(8,128)} async-done(((f32[1024,256]{1,0:T(8,128)}), f32[1024,256]{1,0:T(8,128)}) %all-reduce.10.cloned.1.call-update) | async-done | bytes 1048592 | tf_op jit(solution)/shard_map/psum | solution.py:30
  918.1 2.1 fusion.26
  (125 shorter events, 12.4 us)
Async XLA Ops:
  6.5 323.3 %copy-start = (bf16[8,1280,128]{2,1,0:T(8,128)(2,1)S(1)}, bf16[8,1280,128]{2,1,0:T(8,128)(2,1)}, u32[]{:S(2)}) copy-start(bf16[8,1280,128]{2,1,0:T(8,128)(2,1)} %param.20) | copy-start | bytes 7864324
  6.5 78.8 %copy-start.10 = (f32[256]{0:T(256)S(1)}, f32[256]{0:T(256)}, u32[]{:S(2)}) copy-start(f32[256]{0:T(256)} %param.22) | copy-start | bytes 3076
  6.5 78.8 %all-reduce.6.cloned.1.call-start = ((), (), s32[]{:S(2)}) async-start(), calls=%async_computation.2 | async-start | bytes 1048576 | tf_op jit(solution)/shard_map/psum | solution.py:30
  16.2 71.1 %copy-start.6 = (bf16[256,128]{1,0:T(8,128)(2,1)S(1)}, bf16[256,128]{1,0:T(8,128)(2,1)}, u32[]{:S(2)}) copy-start(bf16[256,128]{1,0:T(8,128)(2,1)} %param.25) | copy-start | bytes 196612
  16.2 71.5 %copy-start.7 = (bf16[256,128]{1,0:T(8,128)(2,1)S(1)}, bf16[256,128]{1,0:T(8,128)(2,1)}, u32[]{:S(2)}) copy-start(bf16[256,128]{1,0:T(8,128)(2,1)} %param.24) | copy-start | bytes 196612
  16.2 310.1 %reduce-scatter.7.cloned.1.call-start = ((), (), s32[]{:S(2)}) async-start(), calls=%async_computation.7 | async-start | bytes 5541888
  85.3 2.0 copy-start.2
  114.5 0.7 copy-start.12
  114.5 1.1 copy-start.19
  114.5 295.0 %all-gather.3.cloned.1.call-start = ((), (), s32[]{:S(2)}) async-start(), calls=%async_computation.3 | async-start | bytes 2162688 | tf_op jit(solution)/shard_map/all_gather | solution.py:53
  115.8 0.9 copy-start.16
  115.8 0.9 copy-start.14
  116.4 0.6 copy-start.17
  327.9 3.1 copy-start.22
  327.9 4.2 copy-start.20
  331.9 77.6 %copy-start.21 = (bf16[1024,256]{1,0:T(8,128)(2,1)S(1)}, bf16[1024,256]{1,0:T(8,128)(2,1)}, u32[]{:S(2)}) copy-start(bf16[1024,256]{1,0:T(8,128)(2,1)} %param.26) | copy-start | bytes 1572868
  333.4 147.1 %copy-start.5 = (bf16[256,1024]{1,0:T(8,128)(2,1)S(1)}, bf16[256,1024]{1,0:T(8,128)(2,1)}, u32[]{:S(2)}) copy-start(bf16[256,1024]{1,0:T(8,128)(2,1)} %param.28) | copy-start | bytes 1572868
  333.4 147.1 %copy-start.11 = (f32[256]{0:T(256)S(1)}, f32[256]{0:T(256)}, u32[]{:S(2)}) copy-start(f32[256]{0:T(256)} %param.27) | copy-start | bytes 3076
  333.4 145.7 %all-reduce.8.cloned.1.call-start = ((), (), s32[]{:S(2)}) async-start(), calls=%async_computation.4 | async-start | bytes 2097152 | tf_op jit(solution)/shard_map/psum | solution.py:30
  412.8 307.8 %reduce-scatter.9.cloned.1.call-start = ((), (), s32[]{:S(2)}) async-start(), calls=%async_computation.8 | async-start | bytes 5541888
  480.5 1.3 copy-start.3
  480.6 0.9 copy-start.8
  480.6 1.2 copy-start.9
  508.6 0.7 copy-start.13
  508.6 213.3 %copy-start.15 = (f32[64]{0:T(128)S(1)}, f32[64]{0:T(128)}, u32[]{:S(2)}) copy-start(f32[64]{0:T(128)} %copy-done.14) | copy-start | bytes 772
  508.6 213.3 %copy-start.18 = (f32[32]{0:T(128)S(1)}, f32[32]{0:T(128)}, u32[]{:S(2)}) copy-start(f32[32]{0:T(128)} %copy-done.17) | copy-start | bytes 388
  508.6 339.8 %all-gather.5.cloned.1.call-start = ((), (), s32[]{:S(2)}) async-start(), calls=%async_computation.5 | async-start | bytes 2162688 | tf_op jit(solution)/shard_map/all_gather | solution.py:53
  771.1 146.9 %copy-start.4 = (bf16[1024,256]{1,0:T(8,128)(2,1)S(1)}, bf16[1024,256]{1,0:T(8,128)(2,1)}, u32[]{:S(2)}) copy-start(bf16[1024,256]{1,0:T(8,128)(2,1)} %copy-done.3) | copy-start | bytes 1572868
  771.8 148.4 %copy-start.1 = (bf16[8,1280,128]{2,1,0:T(8,128)(2,1)S(1)}, bf16[8,1280,128]{2,1,0:T(8,128)(2,1)}, u32[]{:S(2)}) copy-start(bf16[8,1280,128]{2,1,0:T(8,128)(2,1)} %param.20) | copy-start | bytes 7864324
  771.8 146.2 %all-reduce.10.cloned.1.call-start = ((), (), s32[]{:S(2)}) async-start(), calls=%async_computation.6 | async-start | bytes 2097152 | tf_op jit(solution)/shard_map/psum | solution.py:30
Sparse Core Ops, SparseCore 0:
  16.3 68.9 all-reduce.5
  114.6 211.6 reduce-scatter.6
  333.5 75.9 all-gather.2
  412.9 66.1 all-reduce.7
  508.7 211.8 reduce-scatter.8
  771.9 76.3 all-gather.4
  851.9 66.1 all-reduce.9
where the time goes:
time: 928 us; the launch traced here: 927 us
  waiting for transfers between devices  774 us (83%)
  local copies, waits for them, and re-layouts  49.3 us (5%)
  blocking collectives  47.8 us (5%)
  other arithmetic  27.3 us (3%)
  between operations  14 us (2%)
  matrix products  13.9 us (1%)
    unnamed x9, waiting for transfers between devices  420 us
    psum x3, waiting for transfers between devices, width_total(): return lax.psum(partial_value, 'tensor')  201 us
    all_gather x2, waiting for transfers between devices, head_mix(): lax.all_gather(attended, 'rows', axis=0, tiled=True)  153 us
    all_gather x1, blocking collectives, per_device(): lax.all_gather(jnp.concatenate([keys_own, values_own], axis=1), 'rows', a...  47.8 us
  transfers between devices with their start and end apart: 7, of which 7 were waited for; matrix products, arithmetic and copies ran while one was open for 0% of the time, Pallas kernels for 0%

commit v1 on v0

--- a/solution.py
+++ b/solution.py
@@ -50,7 +50,9 @@
 
 def head_mix(attended, matrix):
     return jnp.dot(
-        lax.all_gather(attended, "rows", axis=0, tiled=True),
+        jnp.concatenate(
+            lax.all_to_all(jnp.stack([attended] * lax.axis_size("rows")), "rows", 0, 0), axis=0
+        ),
         matrix,
         preferred_element_type=jnp.float32,
     )

time: 928 us -> 864 us (0.931)
  waiting for transfers between devices: 774 us -> 622 us
  blocking collectives: 47.8 us -> 140 us
    all_gather x2 -> x0, waiting for transfers between devices: 153 us -> none  [head_mix(): lax.all_gather(attended, 'rows', axis=0, tiled=True)]
    all_to_all x0 -> x2, blocking collectives: none -> 90.9 us  [head_mix(): lax.all_to_all(jnp.stack([attended] * lax.axis_size('rows')), 'rows', 0, 0)]
    unnamed x9 -> x7, waiting for transfers between devices: 420 us -> 421 us
  transfers between devices with their start and end apart: 7 -> 5, of which waited for: 7 -> 5; matrix products, arithmetic and copies ran while one was open for 0% -> 0% of each run, Pallas kernels for 0% -> 0%
where the time goes in v1:
time: 864 us; the launch traced here: 863 us
  waiting for transfers between devices  622 us (72%)
  blocking collectives  140 us (16%)
  local copies, waits for them, and re-layouts  48.4 us (6%)
  other arithmetic  27.2 us (3%)
  between operations  13.7 us (2%)
  matrix products  10.7 us (1%)
    unnamed x7, waiting for transfers between devices  421 us
    psum x3, waiting for transfers between devices, width_total(): return lax.psum(partial_value, 'tensor')  202 us
    all_to_all x2, blocking collectives, head_mix(): lax.all_to_all(jnp.stack([attended] * lax.axis_size('rows')), 'rows', 0, 0)  90.9 us
    all_gather x1, blocking collectives, per_device(): lax.all_gather(jnp.concatenate([keys_own, values_own], axis=1), 'rows', a...  49.4 us
  transfers between devices with their start and end apart: 5, of which 5 were waited for; matrix products, arithmetic and copies ran while one was open for 0% of the time, Pallas kernels for 0%

profile of v1, /device:TPU:8, one launch (start us, length us, event | category | flops | bytes accessed | tf_op | source)
XLA Modules:
  0.0 863.2 jit_solution(2034429062263319799)
XLA Ops:
  6.5 0.9 subtract_clamp_fusion
  8.8 6.2 gather_fusion
  15.0 1.1 select_select_fusion
  16.3 69.0 %all-reduce.6.cloned.1.call-done = bf16[1024,256]{1,0:T(8,128)(2,1)} async-done(((bf16[1024,256]{1,0:T(8,128)(2,1)}), bf16[1024,256]{1,0:T(8,128)(2,1)}) %all-reduce.6.cloned.1.call-update) | async-done | bytes 524304 | tf_op jit(solution)/shard_map/psum | solution.py:30
  85.3 2.0 fusion.41
  88.0 2.8 pad_maximum_fusion.2
  90.8 5.9 copy.36
  96.7 5.6 reshape.609
  102.5 5.2 pad_maximum_fusion
  107.7 6.8 reshape.611
  116.8 209.4 %reduce-scatter.7.cloned.1.call-done = f32[1,8,5124]{2,1,0:T(8,128)} async-done(((f32[32,8,5124]{2,1,0:T(8,128)}), f32[1,8,5124]{2,1,0:T(8,128)}) %reduce-scatter.7.cloned.1.call-update) | async-done | bytes 163984
  326.3 1.0 reshape.612
  327.9 0.9 broadcast_multiply_fusion.1
  328.8 0.8 fusion.65
  329.7 1.1 fusion.81
  332.9 52.1 %all_to_all.10 = bf16[32,32,1024]{2,1,0:T(8,128)(2,1)S(1)} all-to-all(bf16[32,32,1024]{2,1,0:T(8,128)(2,1)S(1)} %stack.4), channel_id=1, replica_groups=mesh['rows'=32,'tensor'=8] {'rows'}, dimensions={0} | all-to-all | bytes 4194304 | tf_op jit(solution)/shard_map/all_to_all | solution.py:54
  385.0 1.7 fusion.84
  387.0 66.3 %all-reduce.8.cloned.1.call-done = f32[1024,256]{1,0:T(8,128)} async-done(((f32[1024,256]{1,0:T(8,128)}), f32[1024,256]{1,0:T(8,128)}) %all-reduce.8.cloned.1.call-update) | async-done | bytes 1048592 | tf_op jit(solution)/shard_map/psum | solution.py:30
  453.3 1.4 fusion.25
  454.8 0.8 fusion.35
  456.3 2.9 pad_maximum_fusion.3
  459.2 5.9 copy.37
  465.1 5.6 reshape.620
  470.7 5.2 pad_maximum_fusion.1
  475.9 6.8 reshape.622
  483.7 211.1 %reduce-scatter.9.cloned.1.call-done = f32[1,8,5124]{2,1,0:T(8,128)} async-done(((f32[32,8,5124]{2,1,0:T(8,128)}), f32[1,8,5124]{2,1,0:T(8,128)}) %reduce-scatter.9.cloned.1.call-update) | async-done | bytes 163984
  694.8 1.0 reshape.623
  696.3 49.4 %all_gather.3 = bf16[1024,256]{1,0:T(8,128)(2,1)S(1)} all-gather(bf16[32,256]{1,0:T(8,128)(2,1)S(1)} %pad_maximum_fusion.5), channel_id=1, replica_groups=mesh['rows'=32,'tensor'=8] {'rows'}, dimensions={0}, use_global_device_ids=true | all-gather | bytes 540672 | tf_op jit(solution)/shard_map/all_gather | solution.py:182
  747.4 38.9 %all_to_all.11 = bf16[32,32,1024]{2,1,0:T(8,128)(2,1)S(1)} all-to-all(bf16[32,32,1024]{2,1,0:T(8,128)(2,1)S(1)} %stack.5), channel_id=1, replica_groups=mesh['rows'=32,'tensor'=8] {'rows'}, dimensions={0} | all-to-all | bytes 4194304 | tf_op jit(solution)/shard_map/all_to_all | solution.py:54
  786.2 1.7 fusion.85
  788.0 66.5 %all-reduce.10.cloned.1.call-done = f32[1024,256]{1,0:T(8,128)} async-done(((f32[1024,256]{1,0:T(8,128)}), f32[1024,256]{1,0:T(8,128)}) %all-reduce.10.cloned.1.call-update) | async-done | bytes 1048592 | tf_op jit(solution)/shard_map/psum | solution.py:30
  854.5 2.1 fusion.26
  (125 shorter events, 11.5 us)
Async XLA Ops:
  6.5 323.2 %copy-start = (bf16[8,1280,128]{2,1,0:T(8,128)(2,1)S(1)}, bf16[8,1280,128]{2,1,0:T(8,128)(2,1)}, u32[]{:S(2)}) copy-start(bf16[8,1280,128]{2,1,0:T(8,128)(2,1)} %param.20) | copy-start | bytes 7864324
  6.5 78.8 %copy-start.10 = (f32[256]{0:T(256)S(1)}, f32[256]{0:T(256)}, u32[]{:S(2)}) copy-start(f32[256]{0:T(256)} %param.22) | copy-start | bytes 3076
  6.5 78.8 %all-reduce.6.cloned.1.call-start = ((), (), s32[]{:S(2)}) async-start(), calls=%async_computation.4 | async-start | bytes 1048576 | tf_op jit(solution)/shard_map/psum | solution.py:30
  16.2 71.1 %copy-start.6 = (bf16[256,128]{1,0:T(8,128)(2,1)S(1)}, bf16[256,128]{1,0:T(8,128)(2,1)}, u32[]{:S(2)}) copy-start(bf16[256,128]{1,0:T(8,128)(2,1)} %param.25) | copy-start | bytes 196612
  16.2 71.5 %copy-start.7 = (bf16[256,128]{1,0:T(8,128)(2,1)S(1)}, bf16[256,128]{1,0:T(8,128)(2,1)}, u32[]{:S(2)}) copy-start(bf16[256,128]{1,0:T(8,128)(2,1)} %param.24) | copy-start | bytes 196612
  16.2 310.0 %reduce-scatter.7.cloned.1.call-start = ((), (), s32[]{:S(2)}) async-start(), calls=%async_computation.7 | async-start | bytes 5541888
  85.3 2.0 copy-start.2
  114.4 0.7 copy-start.12
  114.4 1.1 copy-start.19
  114.5 338.8 %all-reduce.8.cloned.1.call-start = ((), (), s32[]{:S(2)}) async-start(), calls=%async_computation.5 | async-start | bytes 2097152 | tf_op jit(solution)/shard_map/psum | solution.py:30
  115.7 0.9 copy-start.16
  115.7 0.9 copy-start.14
  116.3 0.5 copy-start.17
  327.8 3.0 copy-start.23
  327.9 4.1 copy-start.20
  332.6 52.4 %copy-start.21 = (bf16[1024,256]{1,0:T(8,128)(2,1)S(1)}, bf16[1024,256]{1,0:T(8,128)(2,1)}, u32[]{:S(2)}) copy-start(bf16[1024,256]{1,0:T(8,128)(2,1)} %param.26) | copy-start | bytes 1572868
  385.0 69.8 %copy-start.5 = (bf16[256,1024]{1,0:T(8,128)(2,1)S(1)}, bf16[256,1024]{1,0:T(8,128)(2,1)}, u32[]{:S(2)}) copy-start(bf16[256,1024]{1,0:T(8,128)(2,1)} %param.28) | copy-start | bytes 1572868
  385.0 69.8 %copy-start.11 = (f32[256]{0:T(256)S(1)}, f32[256]{0:T(256)}, u32[]{:S(2)}) copy-start(f32[256]{0:T(256)} %param.27) | copy-start | bytes 3076
  386.7 308.1 %reduce-scatter.9.cloned.1.call-start = ((), (), s32[]{:S(2)}) async-start(), calls=%async_computation.8 | async-start | bytes 5541888
  454.7 1.3 copy-start.3
  454.7 0.9 copy-start.8
  454.8 1.2 copy-start.9
  482.7 0.7 copy-start.13
  482.7 213.4 %copy-start.15 = (f32[64]{0:T(128)S(1)}, f32[64]{0:T(128)}, u32[]{:S(2)}) copy-start(f32[64]{0:T(128)} %copy-done.14) | copy-start | bytes 772
  482.7 213.4 %copy-start.18 = (f32[32]{0:T(128)S(1)}, f32[32]{0:T(128)}, u32[]{:S(2)}) copy-start(f32[32]{0:T(128)} %copy-done.17) | copy-start | bytes 388
  482.7 371.8 %all-reduce.10.cloned.1.call-start = ((), (), s32[]{:S(2)}) async-start(), calls=%async_computation.6 | async-start | bytes 2097152 | tf_op jit(solution)/shard_map/psum | solution.py:30
  747.0 39.2 %copy-start.22 = (bf16[1024,256]{1,0:T(8,128)(2,1)S(1)}, bf16[1024,256]{1,0:T(8,128)(2,1)}, u32[]{:S(2)}) copy-start(bf16[1024,256]{1,0:T(8,128)(2,1)} %param.31) | copy-start | bytes 1572868
  786.2 68.3 %copy-start.4 = (bf16[1024,256]{1,0:T(8,128)(2,1)S(1)}, bf16[1024,256]{1,0:T(8,128)(2,1)}, u32[]{:S(2)}) copy-start(bf16[1024,256]{1,0:T(8,128)(2,1)} %copy-done.3) | copy-start | bytes 1572868
  786.2 70.4 %copy-start.1 = (bf16[8,1280,128]{2,1,0:T(8,128)(2,1)S(1)}, bf16[8,1280,128]{2,1,0:T(8,128)(2,1)}, u32[]{:S(2)}) copy-start(bf16[8,1280,128]{2,1,0:T(8,128)(2,1)} %param.20) | copy-start | bytes 7864324
Sparse Core Ops, SparseCore 0:
  16.3 68.9 all-reduce.5
  114.6 211.6 reduce-scatter.6
  386.9 66.3 all-reduce.7
  482.8 211.9 reduce-scatter.8
  788.1 66.3 all-reduce.9
